TPU v7x, 256 devices: a whole 4x4x8 slice. The times are simulated.
256 devices in a mesh: dp: 16 (over y, x_lo, core), feat: 16 (over x_hi, z).
Axes of the slice: x: 4 (x_hi: 2, x_lo: 2; x = x_hi * 2 + x_lo), y: 4, z: 8, core: 2. Of those that a mesh axis runs over, the one named last changes fastest.
Arguments:
- samples: bfloat16 [12288, 256], P('dp'), may hold values from -6 to 6
- targets: bfloat16 [12288], P('dp'), may hold values from -6 to 6
- counts: int32 [16], replicated, may hold values from 1 to 768, 6144 in all
- bucket_ids: int32 [3, 256], replicated, may hold values from 0 to 4095
- sign_bits: int32 [3, 256], replicated, may hold values from 0 to 1
Outputs:
- gram: float32 [4096, 4096], P('dp', 'feat')
- zty: float32 [4096], P('feat')
Inputs may be any that keep to these rules, and one draw needn't show every extreme that they name: The counts sum to 6144, and some index of dp has exactly 768 live rows.
All inputs are finite; a program needn't handle non-finite values.
Results may differ from a plain program's by a relative error of at most 0.0048.
Values may be sent and summed in bfloat16 or wider, within the bound.
A program may use at most 64 MiB of HBM per device.

v0:
```python
import math
import jax
import jax.numpy as jnp
from jax import lax
from jax.sharding import PartitionSpec as P

DIN = 256
SK = 4096
BAL_DEV = 384


def inverse_terms(spectra_pair, freq_ids, column_ids):
    turns = freq_ids[:, None] * column_ids[None, :] % SK
    angles = turns.astype(jnp.float32) * (2.0 * math.pi / SK)
    cosine = jnp.cos(angles).astype(jnp.bfloat16)
    sine = jnp.sin(angles).astype(jnp.bfloat16)
    first_term = jnp.einsum(
        "fc,rf->cr", cosine, spectra_pair[0], preferred_element_type=jnp.float32
    )
    second_term = jnp.einsum("fc,rf->cr", sine, spectra_pair[1], preferred_element_type=jnp.float32)
    return first_term - second_term


def complex_times(real_a, imag_a, real_b, imag_b):
    return (real_a * real_b - imag_a * imag_b, real_a * imag_b + imag_a * real_b)


def body(samples, targets, counts, bucket_ids, sign_bits):
    device_row = lax.axis_index("dp")
    local_count = counts[device_row]
    live_mask = (jnp.arange(samples.shape[0], dtype=jnp.int32) < local_count).astype(jnp.float32)
    values = samples.astype(jnp.float32)
    normed = (
        values
        * lax.rsqrt(jnp.mean(values * values, axis=-1, keepdims=True) + 1e-06)
        * DIN ** (-0.5)
    )
    normed = normed * live_mask[:, None]
    freq_panel = SK // lax.axis_size("feat")
    own_ids = lax.axis_index("feat") * freq_panel + jnp.arange(freq_panel, dtype=jnp.int32)
    turns = bucket_ids[:, :, None] * own_ids[None, None, :] % SK
    angles = turns.astype(jnp.float32) * (2.0 * math.pi / SK)
    signed = (2 * sign_bits - 1).astype(jnp.float32)[:, :, None]
    table = jnp.stack([signed * jnp.cos(angles), -signed * jnp.sin(angles)], axis=1)
    table = jnp.transpose(table, (2, 0, 1, 3)).reshape(DIN, 6 * freq_panel)
    spectrum_all = jnp.dot(
        normed, table, precision=lax.Precision.HIGHEST, preferred_element_type=jnp.float32
    )
    spectrum_all = spectrum_all.reshape(normed.shape[0], 3, 2, freq_panel)
    real_mix, imag_mix = complex_times(
        spectrum_all[:, 0, 0], spectrum_all[:, 0, 1], spectrum_all[:, 1, 0], spectrum_all[:, 1, 1]
    )
    real_mix, imag_mix = complex_times(
        real_mix, imag_mix, spectrum_all[:, 2, 0], spectrum_all[:, 2, 1]
    )
    spectra_pair = jnp.stack([real_mix.astype(jnp.bfloat16), imag_mix.astype(jnp.bfloat16)], axis=0)
    portion = lax.all_gather(spectra_pair, "feat", axis=2, tiled=True)
    freq_ids = jnp.arange(portion.shape[2], dtype=jnp.int32)
    summed = inverse_terms(portion, freq_ids, own_ids)
    features = (summed * SK ** (-0.5)).astype(jnp.bfloat16)
    partial_gram = lax.dot_general(
        lax.all_gather(features, "feat", axis=0, tiled=True),
        features,
        (((1,), (1,)), ((), ())),
        preferred_element_type=jnp.float32,
    )
    gram_local = lax.psum_scatter(partial_gram, "dp", scatter_dimension=0, tiled=True)
    target_part = lax.dot_general(
        features, targets, (((1,), (0,)), ((), ())), preferred_element_type=jnp.float32
    )
    target_sum = lax.psum(target_part, "dp")
    total_rows = BAL_DEV * lax.axis_size("dp")
    return (gram_local / total_rows, target_sum * total_rows ** (-0.5))


def solution(mesh):
    placed = (P("dp", None), P("dp"), P(), P(), P())
    return jax.shard_map(
        body, mesh=mesh, in_specs=placed, out_specs=(P("dp", "feat"), P("feat")), check_vma=False
    )
```

profile of v0, /device:TPU:4, one launch (start us, length us, event | category | flops | bytes accessed | tf_op | source)
XLA Modules:
  0.0 457.0 jit_solution(16290275978402960558)
XLA Ops:
  7.2 0.0 all-gather.3.cloned.1.call-start
  7.2 0.7 add_convert_fusion.1
  7.9 0.7 fusion.37
  8.6 1.2 fusion.16
  9.8 1.2 dynamic_slice.3
  11.0 0.6 add_rsqrt_fusion
  11.7 3.9 cosine_multiply_fusion
  15.6 5.2 %fusion.10 = f32[768,3,2,256]{3,0,2,1:T(8,128)S(1)} fusion(f32[3,1,256,256]{2,3,1,0:T(8,128)S(1)} %get-tuple-element.6, f32[3,1,256,256]{2,3,1,0:T(8,128)S(1)} %get-tuple-element.5, bf16[768,256]{1,0:T(8,128)(2,1)} %param.5, f32[768]{0:T(1024)S(1)} %get-tuple-element.8, f32[768]{0:T(1024)S(1)} %get-tuple-element.7), kind=kOutput, calls=%fused_computation.16 | convolution fusion | flops 3624861696 | bytes 6690816 | tf_op jit(solution)/shard_map/dot_general | solution.py:46
  20.8 0.3 fusion.23
  21.1 0.2 fusion.24
  21.4 1.0 pad_maximum_fusion
  22.4 0.0 all-gather.3.cloned.1.call-update
  22.4 0.0 all-gather.5.cloned.1.call-start
  22.5 193.3 %all-gather.3.cloned.1.call-done = bf16[2,768,4096]{2,1,0:T(8,128)(2,1)} async-done(((bf16[2,768,256]{2,1,0:T(8,128)(2,1)}), bf16[2,768,4096]{2,1,0:T(8,128)(2,1)}) %all-gather.3.cloned.1.call-update) | async-done | bytes 12582928 | tf_op jit(solution)/shard_map/all_gather | solution.py:57
  215.7 0.0 copy-start.2
  215.7 21.5 %fusion = f32[256,768]{1,0:T(8,128)S(1)} fusion(bf16[2,768,4096]{2,1,0:T(8,128)(2,1)} %all-gather.3.cloned.1.call-done, s32[256]{0:T(256)S(1)} %iota_add_fusion), kind=kOutput, calls=%fused_computation.1 | convolution fusion | flops 1626341376 | bytes 7078912 | tf_op jit(solution)/shard_map/fc,rf->cr/dot_general | solution.py:20
  237.2 0.0 copy-done.2
  237.2 21.1 %fusion.15 = bf16[256,768]{1,0:T(8,128)(2,1)} fusion(f32[256,768]{1,0:T(8,128)S(1)} %fusion, bf16[2,768,4096]{2,1,0:T(8,128)(2,1)S(1)} %copy-done.2, s32[256]{0:T(256)S(1)} %iota_add_fusion), kind=kOutput, calls=%fused_computation.24 | convolution fusion | flops 1626931200 | bytes 7472128 | tf_op jit(solution)/shard_map/fc,rf->cr/dot_general | solution.py:17
  258.3 0.0 all-gather.5.cloned.1.call-update
  258.3 0.0 reduce-scatter.2.cloned.1.call-start
  258.4 111.3 %all-gather.5.cloned.1.call-done = bf16[4096,768]{1,0:T(8,128)(2,1)} async-done(((bf16[256,768]{1,0:T(8,128)(2,1)}), bf16[4096,768]{1,0:T(8,128)(2,1)}) %all-gather.5.cloned.1.call-update) | async-done | bytes 6291472 | tf_op jit(solution)/shard_map/all_gather | solution.py:62
  369.7 6.7 %fusion.38 = f32[4096,256]{1,0:T(8,128)} fusion(bf16[4096,768]{1,0:T(8,128)(2,1)} %all-gather.5.cloned.1.call-done, bf16[256,768]{1,0:T(8,128)(2,1)} %fusion.15), kind=kOutput, calls=%fused_computation.63 | convolution fusion | flops 1610612736 | bytes 10878976 | tf_op jit(solution)/shard_map/dot_general | solution.py:61
  376.3 0.0 copy-start.1
  376.3 0.0 copy-start
  376.3 0.0 reduce-scatter.2.cloned.1.call-update
  376.4 0.7 copy-done.1
  377.0 0.3 copy-done
  377.3 0.2 fusion.39
  377.5 29.4 %psum.7 = f32[256]{0:T(256)S(1)} all-reduce(f32[256]{0:T(256)S(1)} %bitcast.36), channel_id=1, replica_groups=mesh['dp'=16,'feat'=16] {'dp'}, use_global_device_ids=true, to_apply=%region_2.3 | all-reduce | flops 256 | bytes 2048 | tf_op jit(solution)/shard_map/psum | solution.py:71
  406.9 0.6 broadcast_multiply_fusion.1
  407.5 41.3 %reduce-scatter.2.cloned.1.call-done = f32[256,256]{1,0:T(8,128)} async-done(((f32[4096,256]{1,0:T(8,128)}), f32[256,256]{1,0:T(8,128)}) %reduce-scatter.2.cloned.1.call-update) | async-done | bytes 262160 | tf_op jit(solution)/shard_map/reduce_scatter | solution.py:67
  448.8 1.7 broadcast_multiply_fusion
  (2 shorter events, 0.0 us)
Async XLA Ops:
  7.2 208.6 %all-gather.3.cloned.1.call-start = ((), (), s32[]{:S(2)}) async-start(), calls=%async_computation.1 | async-start | bytes 13369344 | tf_op jit(solution)/shard_map/all_gather | solution.py:57
  22.4 347.3 %all-gather.5.cloned.1.call-start = ((), (), s32[]{:S(2)}) async-start(), calls=%async_computation.2 | async-start | bytes 6684672 | tf_op jit(solution)/shard_map/all_gather | solution.py:62
  215.7 21.5 %copy-start.2 = (bf16[2,768,4096]{2,1,0:T(8,128)(2,1)S(1)}, bf16[2,768,4096]{2,1,0:T(8,128)(2,1)}, u32[]{:S(2)}) copy-start(bf16[2,768,4096]{2,1,0:T(8,128)(2,1)} %all-gather.3.cloned.1.call-done) | copy-start | bytes 37748740
  258.3 190.5 %reduce-scatter.2.cloned.1.call-start = ((), (), s32[]{:S(2)}) async-start(), calls=%async_computation.3 | async-start | bytes 4456448 | tf_op jit(solution)/shard_map/reduce_scatter | solution.py:67
  376.3 0.7 copy-start.1
  376.3 1.0 copy-start
Sparse Core Ops, SparseCore 0:
  22.5 193.1 all-gather.2
  258.5 111.1 all-gather.4
  376.5 72.3 reduce-scatter.1
where the time goes:
time: 457 us
  waiting for transfers between devices  346 us (76%)
  matrix products  54.6 us (12%)
  blocking collectives  29.4 us (6%)
  between operations  13.8 us (3%)
  other arithmetic  10.9 us (2%)
    all_gather x1, waiting for transfers between devices, body(): portion = lax.all_gather(spectra_pair, 'feat', axis=2, tiled=True)  193 us
    all_gather x1, waiting for transfers between devices, body(): lax.all_gather(features, 'feat', axis=0, tiled=True)  111 us
    reduce_scatter x1, waiting for transfers between devices, body(): lax.psum_scatter(partial_gram, 'dp', scatter_dimension=0, tiled=True)  41.3 us
    psum x1, blocking collectives, body(): target_sum = lax.psum(target_part, 'dp')  29.4 us
    dot_general x1, matrix products, inverse_terms(): jnp.einsum('fc,rf->cr', sine, spectra_pair[1], preferred_element_type=jnp...  21.5 us
    dot_general x1, matrix products, inverse_terms(): jnp.einsum('fc,rf->cr', cosine, spectra_pair[0], preferred_element_type=j...  21.1 us
  transfers between devices with their start and end apart: 3, of which 3 were waited for; matrix products, arithmetic and copies ran while one was open for 0% of the time, Pallas kernels for 0%

commit v1 on v0

--- a/solution.py
+++ b/solution.py
@@ -54,7 +54,9 @@
         real_mix, imag_mix, spectrum_all[:, 2, 0], spectrum_all[:, 2, 1]
     )
     spectra_pair = jnp.stack([real_mix.astype(jnp.bfloat16), imag_mix.astype(jnp.bfloat16)], axis=0)
-    portion = lax.all_gather(spectra_pair, "feat", axis=2, tiled=True)
+    portion = jnp.concatenate(
+        lax.all_to_all(jnp.stack([spectra_pair] * lax.axis_size("feat")), "feat", 0, 0), axis=2
+    )
     freq_ids = jnp.arange(portion.shape[2], dtype=jnp.int32)
     summed = inverse_terms(portion, freq_ids, own_ids)
     features = (summed * SK ** (-0.5)).astype(jnp.bfloat16)

time: 457 us -> 556 us (1.22); the launches traced: 457 us -> 549 us
  blocking collectives: 29.4 us -> 314 us
  waiting for transfers between devices: 346 us -> 153 us
  local copies, waits for them, and re-layouts: 2.23 us -> 11.9 us
  matrix products: 54.6 us -> 45 us
    all_to_all x0 -> x1, blocking collectives: none -> 284 us  [body(): lax.all_to_all(jnp.stack([spectra_pair] * lax.axis_size('feat')), 'feat',...]
    all_gather x1 -> x0, waiting for transfers between devices: 193 us -> none  [body(): portion = lax.all_gather(spectra_pair, 'feat', axis=2, tiled=True)]
    another operation x0 -> x2, local copies, waits for them, and re-layouts: none -> 6.24 us  [the longest x1 5.97 us: body(): jnp.stack([spectra_pair] * lax.axis_size('feat'))]
  transfers between devices with their start and end apart: 3 -> 2, of which waited for: 3 -> 2; matrix products, arithmetic and copies ran while one was open for 0% -> 0% of each run, Pallas kernels for 0% -> 0%
where the time goes in v1:
time: 556 us; the launch traced here: 549 us
  blocking collectives  314 us (56%)
  waiting for transfers between devices  153 us (28%)
  matrix products  45 us (8%)
  between operations  14.5 us (3%)
  local copies, waits for them, and re-layouts  11.9 us (2%)
  other arithmetic  9.97 us (2%)
    all_to_all x1, blocking collectives, body(): lax.all_to_all(jnp.stack([spectra_pair] * lax.axis_size('feat')), 'feat',...  284 us
    all_gather x1, waiting for transfers between devices, body(): lax.all_gather(features, 'feat', axis=0, tiled=True)  112 us
    reduce_scatter x1, waiting for transfers between devices, body(): lax.psum_scatter(partial_gram, 'dp', scatter_dimension=0, tiled=True)  41.4 us
    psum x1, blocking collectives, body(): target_sum = lax.psum(target_part, 'dp')  29.4 us
    dot_general x1, matrix products, inverse_terms(): jnp.einsum('fc,rf->cr', sine, spectra_pair[1], preferred_element_type=jnp...  17 us
    dot_general x1, matrix products, inverse_terms(): jnp.einsum('fc,rf->cr', cosine, spectra_pair[0], preferred_element_type=j...  16 us
  transfers between devices with their start and end apart: 2, of which 2 were waited for; matrix products, arithmetic and copies ran while one was open for 0% of the time, Pallas kernels for 0%

profile of v1, /device:TPU:4, one launch (start us, length us, event | category | flops | bytes accessed | tf_op | source)
XLA Modules:
  0.0 548.7 jit_solution(1466950316680845276)
XLA Ops:
  7.2 0.0 all-gather.2.cloned.1.call-start
  7.2 0.7 add_convert_fusion.1
  7.9 0.7 fusion.37
  8.6 1.2 fusion.16
  9.8 1.2 dynamic_slice.3
  11.0 0.6 add_rsqrt_fusion
  11.7 3.9 cosine_multiply_fusion
  15.6 5.2 fusion.10
  20.8 0.3 fusion.23
  21.1 0.2 fusion.24
  21.4 0.1 pad_maximum_fusion
  21.5 0.3 copy.8
  21.7 6.0 %stack.8 = bf16[16,2,768,256]{2,3,1,0:T(8,128)(2,1)} broadcast(bf16[2,768,256]{1,2,0:T(8,128)(2,1)S(1)} %copy.8), dimensions={1,2,3} | broadcast | bytes 13369344 | tf_op jit(solution)/shard_map/stack | solution.py:58
  27.7 284.3 %all_to_all.5 = bf16[16,2,768,256]{2,3,1,0:T(8,128)(2,1)S(1)} all-to-all(bf16[16,2,768,256]{2,3,1,0:T(8,128)(2,1)} %stack.8), channel_id=1, replica_groups=mesh['dp'=16,'feat'=16] {'feat'}, dimensions={0} | all-to-all | bytes 25165824 | tf_op jit(solution)/shard_map/all_to_all | solution.py:58
  312.0 1.9 copy.12
  314.0 1.5 fusion.38
  315.5 16.0 %fusion.6 = f32[256,768]{1,0:T(8,128)S(1)} fusion(bf16[768,4096]{0,1:T(8,128)(2,1)S(1)} %bitcast.33, s32[256]{0:T(256)S(1)} %iota_add_fusion), kind=kOutput, calls=%fused_computation.12 | convolution fusion | flops 1626341376 | bytes 7078912 | tf_op jit(solution)/shard_map/fc,rf->cr/dot_general | solution.py:17
  331.5 17.0 %fusion.15 = bf16[256,768]{1,0:T(8,128)(2,1)} fusion(f32[256,768]{1,0:T(8,128)S(1)} %fusion.6, bf16[768,4096]{0,1:T(8,128)(2,1)S(1)} %bitcast.32, s32[256]{0:T(256)S(1)} %iota_add_fusion), kind=kOutput, calls=%fused_computation.23 | convolution fusion | flops 1626931200 | bytes 7472128 | tf_op jit(solution)/shard_map/fc,rf->cr/dot_general | solution.py:20
  348.5 0.0 all-gather.2.cloned.1.call-update
  348.5 0.0 reduce-scatter.2.cloned.1.call-start
  348.6 112.0 %all-gather.2.cloned.1.call-done = bf16[4096,768]{1,0:T(8,128)(2,1)} async-done(((bf16[256,768]{1,0:T(8,128)(2,1)}), bf16[4096,768]{1,0:T(8,128)(2,1)}) %all-gather.2.cloned.1.call-update) | async-done | bytes 6291472 | tf_op jit(solution)/shard_map/all_gather | solution.py:64
  460.6 6.7 %fusion.39 = f32[4096,256]{1,0:T(8,128)} fusion(bf16[4096,768]{1,0:T(8,128)(2,1)} %all-gather.2.cloned.1.call-done, bf16[256,768]{1,0:T(8,128)(2,1)} %fusion.15), kind=kOutput, calls=%fused_computation.63 | convolution fusion | flops 1610612736 | bytes 10878976 | tf_op jit(solution)/shard_map/dot_general | solution.py:63
  467.3 0.0 copy-start.1
  467.3 0.0 copy-start
  467.3 0.0 reduce-scatter.2.cloned.1.call-update
  467.3 0.7 copy-done.1
  467.9 0.3 copy-done
  468.3 0.2 fusion.40
  468.4 29.4 %psum.7 = f32[256]{0:T(256)S(1)} all-reduce(f32[256]{0:T(256)S(1)} %bitcast.34), channel_id=1, replica_groups=mesh['dp'=16,'feat'=16] {'dp'}, use_global_device_ids=true, to_apply=%region_2.3 | all-reduce | flops 256 | bytes 2048 | tf_op jit(solution)/shard_map/psum | solution.py:73
  497.9 0.6 broadcast_multiply_fusion.1
  498.4 41.4 %reduce-scatter.2.cloned.1.call-done = f32[256,256]{1,0:T(8,128)} async-done(((f32[4096,256]{1,0:T(8,128)}), f32[256,256]{1,0:T(8,128)}) %reduce-scatter.2.cloned.1.call-update) | async-done | bytes 262160 | tf_op jit(solution)/shard_map/reduce_scatter | solution.py:69
  539.8 1.7 broadcast_multiply_fusion
  (2 shorter events, 0.0 us)
Async XLA Ops:
  7.2 453.4 %all-gather.2.cloned.1.call-start = ((), (), s32[]{:S(2)}) async-start(), calls=%async_computation.2 | async-start | bytes 6684672 | tf_op jit(solution)/shard_map/all_gather | solution.py:64
  348.5 191.3 %reduce-scatter.2.cloned.1.call-start = ((), (), s32[]{:S(2)}) async-start(), calls=%async_computation.3 | async-start | bytes 4456448 | tf_op jit(solution)/shard_map/reduce_scatter | solution.py:69
  467.3 0.7 copy-start.1
  467.3 1.0 copy-start
Sparse Core Ops, SparseCore 0:
  348.6 111.9 all-gather.1
  467.4 72.3 reduce-scatter.1
